TPU v7x, 32 devices: a whole 2x2x4 slice. The times are simulated.
32 devices in a mesh: dp: 8 (over z, x), row: 2 (over y), col: 2 (over core).
Axes of the slice: x: 2, y: 2, z: 4, core: 2. Of those that a mesh axis runs over, the one named last changes fastest.
Arguments:
- block_input: float32 [4096, 640], P(('dp', 'col'), 'row'), may hold values from -200 to 200
- segment_ids: int32 [16, 256], P(('dp', 'row')), may hold values from 0 to 3, never falling along the last dimension, each value on 1 to 128 neighbouring positions
- w_query: bfloat16 [640, 1024], P('row', 'col'), may hold values from -0.25 to 0.25
- w_key: bfloat16 [640, 256], P('row'), may hold values from -0.25 to 0.25
- w_value: bfloat16 [640, 256], P('row'), may hold values from -0.25 to 0.25
- w_out: bfloat16 [1024, 640], P('col', 'row'), may hold values from -0.1875 to 0.1875
- w_gate: bfloat16 [640, 2048], P('row', 'col'), may hold values from -0.25 to 0.25
- w_up: bfloat16 [640, 2048], P('row', 'col'), may hold values from -0.25 to 0.25
- w_down: bfloat16 [2048, 640], P('col', 'row'), may hold values from -0.125 to 0.125
- gain_input: float32 [640], P('row'), may hold values from 0.25 to 1.75
- gain_attn: float32 [640], P('row'), may hold values from 0.25 to 1.75
- gain_ffn_pre: float32 [640], P('row'), may hold values from 0.25 to 1.75
- gain_ffn_post: float32 [640], P('row'), may hold values from 0.25 to 1.75
- gain_query: float32 [256], replicated, may hold values from 0.25 to 1.75
- gain_key: float32 [256], replicated, may hold values from 0.25 to 1.75
- out_cotangent: float32 [4096, 640], P(('dp', 'col'), 'row'), may hold values from -6 to 6
Outputs:
- block_output: float32 [4096, 640], P(('dp', 'col'), 'row')
- input_grad: float32 [4096, 640], P(('dp', 'col'), 'row')
- query_grad: float32 [640, 1024], P('row', 'col')
- key_grad: float32 [640, 256], P('row')
- value_grad: float32 [640, 256], P('row')
- out_grad: float32 [1024, 640], P('col', 'row')
- gate_grad: float32 [640, 2048], P('row', 'col')
- up_grad: float32 [640, 2048], P('row', 'col')
- down_grad: float32 [2048, 640], P('col', 'row')
- gain_input_grad: float32 [640], P('row')
- gain_attn_grad: float32 [640], P('row')
- gain_ffn_pre_grad: float32 [640], P('row')
- gain_ffn_post_grad: float32 [640], P('row')
- gain_query_grad: float32 [256], replicated
- gain_key_grad: float32 [256], replicated
Inputs may be any that keep to these rules, and one draw needn't show every extreme that they name: `segment_ids`: one packed sequence a row; document numbers never fall, start at 0 and take every value up to 3; each document has 1 to 128 tokens and one has exactly 128.
All inputs are finite; a program needn't handle non-finite values.
Results may differ from a plain program's by a relative error of at most 0.014.
Values may be sent and summed in bfloat16 or wider, within the bound.
No kernel may reach another device: no remote copies, remote signals or barrier semaphores. Data moves between devices by JAX's collectives and lax.ppermute only.
A program may use at most 64 MiB of HBM per device.

v0:
```python
import jax
import jax.numpy as jnp
from jax import lax
from jax.sharding import PartitionSpec as P

D = 640
HD = 256
eps_norm = 1e-06
rope_base = 1000000.0


def rms_scale(values):
    return lax.rsqrt(jnp.mean(values * values, axis=-1, keepdims=True) + eps_norm)


def rope_tables(segments):
    length = segments.shape[-1]
    places = jnp.arange(length, dtype=jnp.int32)
    earlier = jnp.concatenate([segments[..., :1] - 1, segments[..., :-1]], axis=-1)
    starts = lax.cummax(jnp.where(segments != earlier, places, 0), axis=segments.ndim - 1)
    offsets = (places - starts).astype(jnp.float32)
    frequency = rope_base ** (-(jnp.arange(HD // 2, dtype=jnp.float32) * 2.0 / HD))
    angles = offsets[..., None] * frequency
    return (jnp.cos(angles), jnp.sin(angles))


def rotate(values, cosine_table, sine_table):
    lower_half = values[..., : HD // 2]
    upper_half = values[..., HD // 2 :]
    return jnp.concatenate(
        [
            lower_half * cosine_table - upper_half * sine_table,
            upper_half * cosine_table + lower_half * sine_table,
        ],
        axis=-1,
    )


def gelu_tanh(values):
    return jax.nn.gelu(values, approximate=True)


def width_total(values):
    return lax.psum(values, "row")


def norm_forward(values, gain_vector):
    squares = width_total(jnp.sum(values * values, axis=1, keepdims=True))
    inv_rms = lax.rsqrt(squares / D + eps_norm)
    return (values * inv_rms * gain_vector, inv_rms)


def norm_backward(upstream, values, inv_rms, gain_vector):
    weighted = upstream * gain_vector
    width_sum = width_total(jnp.sum(weighted * values, axis=1, keepdims=True))
    through = inv_rms * weighted - values * inv_rms**3 * width_sum / D
    return (through, jnp.sum(upstream * values * inv_rms, axis=0))


def token_gather(values):
    return lax.all_gather(values, "col", axis=0, tiled=True)


def hidden_gather(values):
    return lax.all_gather(values, "row", axis=0, tiled=True)


def rows_term(gathered, weight, contract):
    return lax.dot_general(
        gathered, weight, (((1,), (contract,)), ((), ())), preferred_element_type=jnp.float32
    )


def project_sum(gathered, weight, contract):
    return lax.psum_scatter(
        rows_term(gathered, weight, contract), "row", scatter_dimension=0, tiled=True
    )


def column_sum(gathered, weight, contract):
    return lax.psum_scatter(
        rows_term(gathered, weight, contract), "col", scatter_dimension=0, tiled=True
    )


def weight_term(left, right):
    return lax.dot_general(
        left, right, (((0,), (0,)), ((), ())), preferred_element_type=jnp.float32
    )


def attention_forward(query_bf, key_bf, value_bf, allowed, logit_scale_factor):
    seq_rows, head_count = (query_bf.shape[0], query_bf.shape[1])
    block_rows = min(512, seq_rows)
    block_count = seq_rows // block_rows
    query_blocks = query_bf.reshape(block_count, block_rows, head_count, HD)
    mask_blocks = allowed.reshape(block_count, block_rows, seq_rows)

    def one_block(operands):
        query_part, mask_part = operands
        attention_logits = (
            jnp.einsum("qhd,kd->hqk", query_part, key_bf, preferred_element_type=jnp.float32)
            * logit_scale_factor
        )
        weights = jnp.where(mask_part[None], jnp.exp(attention_logits), 0.0)
        row_total = jnp.sum(weights, axis=2, keepdims=True)
        probabilities = (weights / row_total).astype(jnp.bfloat16)
        mixed_head_outputs = jnp.einsum(
            "hqk,kd->qhd", probabilities, value_bf, preferred_element_type=jnp.float32
        )
        return (mixed_head_outputs, jnp.log(row_total))

    mixed_head_outputs, log_total = lax.map(one_block, (query_blocks, mask_blocks))
    return (mixed_head_outputs.reshape(seq_rows, head_count * HD), log_total)


def attention_backward(
    query_bf, key_bf, value_bf, allowed, logit_scale_factor, log_total, grad_heads_bf
):
    seq_rows, head_count = (query_bf.shape[0], query_bf.shape[1])
    block_rows = min(512, seq_rows)
    block_count = seq_rows // block_rows
    query_blocks = query_bf.reshape(block_count, block_rows, head_count, HD)
    grad_blocks = grad_heads_bf.reshape(block_count, block_rows, head_count, HD)
    mask_blocks = allowed.reshape(block_count, block_rows, seq_rows)

    def one_block(running, operands):
        key_acc, value_acc = running
        query_part, mask_part, lse_part, grad_part = operands
        attention_logits = (
            jnp.einsum("qhd,kd->hqk", query_part, key_bf, preferred_element_type=jnp.float32)
            * logit_scale_factor
        )
        probabilities = jnp.where(mask_part[None], jnp.exp(attention_logits - lse_part), 0.0)
        prob_bf = probabilities.astype(jnp.bfloat16)
        value_acc = value_acc + jnp.einsum(
            "hqk,qhd->kd", prob_bf, grad_part, preferred_element_type=jnp.float32
        )
        probability_gradient = jnp.einsum(
            "qhd,kd->hqk", grad_part, value_bf, preferred_element_type=jnp.float32
        )
        row_delta = jnp.sum(probabilities * probability_gradient, axis=2, keepdims=True)
        score_gradient = (probabilities * (probability_gradient - row_delta)).astype(jnp.bfloat16)
        grad_query = (
            jnp.einsum("hqk,kd->qhd", score_gradient, key_bf, preferred_element_type=jnp.float32)
            * logit_scale_factor
        )
        key_acc = (
            key_acc
            + jnp.einsum(
                "hqk,qhd->kd", score_gradient, query_part, preferred_element_type=jnp.float32
            )
            * logit_scale_factor
        )
        return ((key_acc, value_acc), grad_query)

    zero_rows = jnp.zeros((seq_rows, HD), jnp.float32)
    (grad_key, grad_value), grad_query = lax.scan(
        one_block, (zero_rows, zero_rows), (query_blocks, mask_blocks, log_total, grad_blocks)
    )
    return (grad_query.reshape(seq_rows, head_count, HD), grad_key, grad_value)


def on_device(
    block_input,
    segment_ids,
    w_query,
    w_key,
    w_value,
    w_out,
    w_gate,
    w_up,
    w_down,
    gain_input,
    gain_attn,
    gain_ffn_pre,
    gain_ffn_post,
    gain_query,
    gain_key,
    out_cotangent,
):
    seq_rows = block_input.shape[0]
    query_width = w_query.shape[1]
    head_count = query_width // HD
    hidden_width = w_gate.shape[1]
    logit_scale_factor = HD ** (-0.5)
    segments = segment_ids[0]
    cosine_table, sine_table = rope_tables(segments)
    places = jnp.arange(seq_rows, dtype=jnp.int32)
    allowed = (segments[:, None] == segments[None, :]) & (places[:, None] >= places[None, :])

    def query_map(unnormed, gain_vector):
        return rotate(
            unnormed * rms_scale(unnormed) * gain_vector,
            cosine_table[:, None, :],
            sine_table[:, None, :],
        )

    def key_map(unnormed, gain_vector):
        return rotate(unnormed * rms_scale(unnormed) * gain_vector, cosine_table, sine_table)

    normed_in, scale_in = norm_forward(block_input, gain_input)
    input_all = token_gather(normed_in.astype(jnp.bfloat16))
    joint_weight = jnp.concatenate([w_query, w_key, w_value], axis=1)
    projected = project_sum(input_all, joint_weight, 0)
    raw_query = projected[:, :query_width].reshape(seq_rows, head_count, HD)
    raw_key = projected[:, query_width : query_width + HD]
    raw_value = projected[:, query_width + HD :]
    query_bf = query_map(raw_query, gain_query).astype(jnp.bfloat16)
    key_bf = key_map(raw_key, gain_key).astype(jnp.bfloat16)
    value_bf = raw_value.astype(jnp.bfloat16)
    mixed_head_outputs, log_total = attention_forward(
        query_bf, key_bf, value_bf, allowed, logit_scale_factor
    )
    heads_all = lax.all_gather(mixed_head_outputs.astype(jnp.bfloat16), "row", axis=0, tiled=True)
    attn_proj = column_sum(heads_all, w_out, 0)
    attn_normed, scale_y = norm_forward(attn_proj, gain_attn)
    resid_mid = block_input + attn_normed
    ffn_normed, scale_mid = norm_forward(resid_mid, gain_ffn_pre)
    ffn_all = token_gather(ffn_normed.astype(jnp.bfloat16))
    mix_weight = jnp.concatenate([w_gate, w_up], axis=1)
    gate_up = lax.psum_scatter(
        rows_term(ffn_all, mix_weight, 0), "row", scatter_dimension=0, tiled=True
    )
    gate_value = gate_up[:, :hidden_width]
    up_value = gate_up[:, hidden_width:]
    gelu_value, gelu_pull = jax.vjp(gelu_tanh, gate_value)
    hidden_all = hidden_gather((gelu_value * up_value).astype(jnp.bfloat16))
    ffn_out = column_sum(hidden_all, w_down, 0)
    ffn_normed_out, scale_f = norm_forward(ffn_out, gain_ffn_post)
    block_output = resid_mid + ffn_normed_out
    grad_ffn, post_part = norm_backward(out_cotangent, ffn_out, scale_f, gain_ffn_post)
    grad_ffn_all = token_gather(grad_ffn.astype(jnp.bfloat16))
    grad_hidden = project_sum(grad_ffn_all, w_down, 1)
    down_grad = weight_term(hidden_all, grad_ffn_all)
    grad_gate = gelu_pull(grad_hidden * up_value)[0]
    grad_up = grad_hidden * gelu_value
    grad_mix = jnp.concatenate([grad_gate, grad_up], axis=1).astype(jnp.bfloat16)
    grad_mix_all = lax.all_gather(grad_mix, "row", axis=0, tiled=True)
    grad_pre = column_sum(grad_mix_all, mix_weight, 1)
    mix_grad = weight_term(ffn_all, grad_mix_all)
    grad_mid_norm, pre_part = norm_backward(grad_pre, resid_mid, scale_mid, gain_ffn_pre)
    grad_mid = out_cotangent + grad_mid_norm
    grad_attn, attn_part = norm_backward(grad_mid, attn_proj, scale_y, gain_attn)
    grad_attn_all = token_gather(grad_attn.astype(jnp.bfloat16))
    grad_heads = lax.psum_scatter(
        rows_term(grad_attn_all, w_out, 1), "row", scatter_dimension=0, tiled=True
    )
    out_grad = weight_term(heads_all, grad_attn_all)
    grad_heads_bf = grad_heads.astype(jnp.bfloat16).reshape(seq_rows, head_count, HD)
    rotated_query_gradient, grad_key_rot, grad_value = attention_backward(
        query_bf, key_bf, value_bf, allowed, logit_scale_factor, log_total, grad_heads_bf
    )
    query_pull = jax.vjp(query_map, raw_query, gain_query)[1]
    grad_raw_query, query_gain_part = query_pull(rotated_query_gradient)
    key_pull = jax.vjp(key_map, raw_key, gain_key)[1]
    grad_raw_key, key_gain_part = key_pull(grad_key_rot)
    grad_joint = jnp.concatenate(
        [grad_raw_query.reshape(seq_rows, query_width), grad_raw_key, grad_value], axis=1
    ).astype(jnp.bfloat16)
    grad_joint_all = hidden_gather(grad_joint)
    grad_in = column_sum(grad_joint_all, joint_weight, 1)
    joint_grad = weight_term(input_all, grad_joint_all)
    grad_x_norm, input_part = norm_backward(grad_in, block_input, scale_in, gain_input)
    input_grad = grad_mid + grad_x_norm
    query_part_grad = joint_grad[:, :query_width]
    key_part_grad = joint_grad[:, query_width : query_width + HD]
    value_part_grad = joint_grad[:, query_width + HD :]
    query_sum, out_sum_grad, mix_sum, down_sum = lax.psum(
        (query_part_grad, out_grad, mix_grad, down_grad), "dp"
    )
    key_sum, value_sum, input_gain_sum, attn_gain_sum, pre_gain_sum, post_gain_sum = lax.psum(
        (key_part_grad, value_part_grad, input_part, attn_part, pre_part, post_part), ("dp", "col")
    )
    query_gain_sum, key_gain_sum = lax.psum((query_gain_part, key_gain_part), ("dp", "row", "col"))
    return (
        block_output,
        input_grad,
        query_sum,
        key_sum,
        value_sum,
        out_sum_grad,
        mix_sum[:, :hidden_width],
        mix_sum[:, hidden_width:],
        down_sum,
        input_gain_sum,
        attn_gain_sum,
        pre_gain_sum,
        post_gain_sum,
        query_gain_sum,
        key_gain_sum,
    )


def solution(mesh):
    placed = (
        P(("dp", "col"), "row"),
        P(("dp", "row"), None),
        P("row", "col"),
        P("row", None),
        P("row", None),
        P("col", "row"),
        P("row", "col"),
        P("row", "col"),
        P("col", "row"),
        P("row"),
        P("row"),
        P("row"),
        P("row"),
        P(),
        P(),
        P(("dp", "col"), "row"),
    )
    return jax.shard_map(
        on_device,
        mesh=mesh,
        in_specs=placed,
        out_specs=(
            P(("dp", "col"), "row"),
            P(("dp", "col"), "row"),
            P("row", "col"),
            P("row", None),
            P("row", None),
            P("col", "row"),
            P("row", "col"),
            P("row", "col"),
            P("col", "row"),
            P("row"),
            P("row"),
            P("row"),
            P("row"),
            P(),
            P(),
        ),
        check_vma=False,
    )
```

profile of v0, /device:TPU:0, one launch (start us, length us, event | category | flops | bytes accessed | tf_op | source)
XLA Modules:
  0.0 678.4 jit_solution(7398071400886092553)
XLA Ops:
  7.3 1.1 multiply_reduce_fusion.14
  8.4 5.9 psum.140
  14.8 1.1 multiply_convert_fusion.4
  15.9 2.0 all_gather.24
  18.0 1.1 constant_dynamic-update-slice_fusion.2
  20.9 2.1 fusion.50
  25.1 31.8 %reduce-scatter.9.cloned.1.call-done = f32[256,1024]{1,0:T(8,128)} async-done(((f32[512,1024]{1,0:T(8,128)}), f32[256,1024]{1,0:T(8,128)}) %reduce-scatter.9.cloned.1.call-update) | async-done | bytes 1048592 | tf_op jit(solution)/shard_map/reduce_scatter | solution.py:75
  56.8 1.1 multiply_reduce_fusion.17
  58.0 1.1 slice.83
  62.4 8.5 %all_gather.25 = bf16[512,512]{0,1:T(8,128)(2,1)S(1)} all-gather(bf16[256,512]{0,1:T(8,128)(2,1)S(1)} %bitcast.105), channel_id=1, replica_groups=mesh['dp'=8,'row'=2,'col'=2] {'row'}, dimensions={0}, use_global_device_ids=true | all-gather | bytes 786432 | tf_op jit(solution)/shard_map/all_gather | solution.py:215
  71.8 1.2 fusion.59
  73.0 1.2 constant_dynamic-update-slice_fusion.4
  74.2 1.1 constant_dynamic-update-slice_fusion.3
  75.4 5.8 reduce-scatter.11.cloned.1.call-done
  82.2 4.9 psum.141
  87.1 1.1 multiply_reduce_fusion.12
  88.2 4.9 psum.142
  93.3 2.0 all_gather.26
  96.1 3.2 fusion.51
  99.4 55.6 %reduce-scatter.13.cloned.1.call-done = f32[256,2048]{1,0:T(8,128)} async-done(((f32[512,2048]{1,0:T(8,128)}), f32[256,2048]{1,0:T(8,128)}) %reduce-scatter.13.cloned.1.call-update) | async-done | bytes 2097168 | tf_op jit(solution)/shard_map/reduce_scatter | solution.py:222
  155.0 2.7 multiply_convert_fusion.1
  157.8 21.4 %all-gather.4.cloned.1.call-done = bf16[512,1024]{1,0:T(8,128)(2,1)} async-done(((bf16[256,1024]{1,0:T(8,128)(2,1)}), bf16[512,1024]{1,0:T(8,128)(2,1)}) %all-gather.4.cloned.1.call-update) | async-done | bytes 1048592 | tf_op jit(solution)/shard_map/all_gather | solution.py:65
  179.2 2.6 fusion.52
  181.8 8.1 %reduce-scatter.15.cloned.1.call-done = f32[256,320]{0,1:T(8,128)} async-done(((f32[512,320]{0,1:T(8,128)}), f32[256,320]{0,1:T(8,128)}) %reduce-scatter.15.cloned.1.call-update) | async-done | bytes 327696 | tf_op jit(solution)/shard_map/reduce_scatter | solution.py:81
  191.0 4.9 psum.143
  196.0 1.8 multiply_reduce_fusion.3
  197.7 4.9 psum.144
  202.6 1.8 subtract_convert_fusion.1
  204.5 2.0 all_gather.28
  207.2 2.1 fusion.53
  209.4 33.1 %reduce-scatter.17.cloned.1.call-done = f32[256,1024]{1,0:T(8,128)} async-done(((f32[512,1024]{1,0:T(8,128)}), f32[256,1024]{1,0:T(8,128)}) %reduce-scatter.17.cloned.1.call-update) | async-done | bytes 1048592 | tf_op jit(solution)/shard_map/reduce_scatter | solution.py:75
  242.5 2.0 fusion.10
  245.7 33.2 %all-gather.6.cloned.1.call-done = bf16[512,2048]{1,0:T(8,128)(2,1)} async-done(((bf16[256,2048]{1,0:T(8,128)(2,1)}), bf16[512,2048]{1,0:T(8,128)(2,1)}) %all-gather.6.cloned.1.call-update) | async-done | bytes 2097168 | tf_op jit(solution)/shard_map/all_gather | solution.py:239
  278.9 3.3 fusion.54
  282.3 8.1 %reduce-scatter.19.cloned.1.call-done = f32[256,320]{0,1:T(8,128)} async-done(((f32[512,320]{0,1:T(8,128)}), f32[256,320]{0,1:T(8,128)}) %reduce-scatter.19.cloned.1.call-update) | async-done | bytes 327696 | tf_op jit(solution)/shard_map/reduce_scatter | solution.py:81
  290.4 1.8 multiply_reduce_fusion.4
  292.2 4.9 psum.145
  297.1 1.8 multiply_reduce_fusion.5
  298.9 5.0 psum.146
  304.1 2.0 all_gather.30
  306.1 2.5 fusion.55
  308.9 21.4 %reduce-scatter.21.cloned.1.call-done = f32[256,512]{1,0:T(8,128)} async-done(((f32[512,512]{1,0:T(8,128)}), f32[256,512]{1,0:T(8,128)}) %reduce-scatter.21.cloned.1.call-update) | async-done | bytes 524304 | tf_op jit(solution)/shard_map/reduce_scatter | solution.py:246
  330.3 1.8 convert_element_type.61
  332.1 1.8 copy.129
  333.9 1.9 fusion.3
  335.8 1.2 multiply_reduce_fusion.1
  339.9 1.7 copy.116
  343.9 2.0 pad_maximum_fusion.1
  346.0 21.4 %all-gather.8.cloned.1.call-done = bf16[512,1024]{0,1:T(8,128)(2,1)} async-done(((bf16[256,1024]{0,1:T(8,128)(2,1)}), bf16[512,1024]{0,1:T(8,128)(2,1)}) %all-gather.8.cloned.1.call-update) | async-done | bytes 1048592 | tf_op jit(solution)/shard_map/all_gather | solution.py:65
  367.4 2.6 fusion.60
  370.1 1.6 fusion.61
  371.9 2.4 fusion.58
  374.3 1.2 fusion.57
  377.6 44.1 %all-reduce.4 = (f32[256]{0:T(256)}, f32[256]{0:T(256)}) all-reduce(f32[256]{0:T(256)S(1)} %get-tuple-element.68, f32[256]{0:T(256)S(1)} %copy-done.62), channel_id=1, replica_groups=mesh['dp'=8,'row'=2,'col'=2] {'dp','row','col'}, use_global_device_ids=true, to_apply=%region_47.48 | all-reduce | flops 512 | bytes 4096 | tf_op jit(solution)/shard_map/psum | solution.py:275
  422.7 1.2 multiply_reduce_fusion.6
  423.8 5.4 psum.147
  429.3 1.8 subtract_add_fusion
  431.1 33.6 %all-reduce.5 = (f32[320]{0:T(512)}, f32[320]{0:T(512)}, f32[320]{0:T(512)}, f32[320]{0:T(512)}) all-reduce(f32[320]{0:T(512)S(1)} %get-tuple-element.76, f32[320]{0:T(512)S(1)} %copy-done.61, f32[320]{0:T(512)S(1)} %copy-done.60, f32[320]{0:T(512)S(1)} %copy-done.59), channel_id=1, replica_groups=mesh['dp'=8,'row'=2,'col'=2] {'dp','col'}, use_global_device_ids=true, to_apply=%region_39.40 | all-reduce | flops 1280 | bytes 10240 | tf_op jit(solution)/shard_map/psum | solution.py:272
  464.7 105.0 %all-reduce.13.cloned.1.call-done = (f32[320,512]{1,0:T(8,128)}, f32[512,320]{0,1:T(8,128)}, f32[320,2048]{1,0:T(8,128)}, f32[1024,320]{0,1:T(8,128)}) async-done(((f32[320,512]{1,0:T(8,128)}, f32[512,320]{0,1:T(8,128)}, f32[320,2048]{1,0:T(8,128)}, f32[1024,320]{0,1:T(8,128)}), (f32[320,512]{1,0:T(8,128)}, f32[512,320]{0,1:T(8,128)}, f32[320,2048]{1,0:T(8,128)}, ...) | async-done | bytes 5242896 | tf_op jit(solution)/shard_map/psum | solution.py:269
  569.7 3.5 fusion.48
  573.3 91.3 %all-reduce.11.cloned.1.call-done = (f32[320,256]{1,0:T(8,128)}, f32[320,256]{1,0:T(8,128)}) async-done(((f32[320,256]{1,0:T(8,128)}, f32[320,256]{1,0:T(8,128)}), (f32[320,256]{1,0:T(8,128)}, f32[320,256]{1,0:T(8,128)})) %all-reduce.11.cloned.1.call-update) | async-done | bytes 655376 | tf_op jit(solution)/shard_map/psum | solution.py:272
  664.6 2.0 copy.144
  666.6 1.7 copy.145
  668.3 1.7 copy.146
  (212 shorter events, 23.7 us)
Async XLA Ops:
  7.2 172.0 %copy-start = (bf16[1024,320]{0,1:T(8,128)(2,1)S(1)}, bf16[1024,320]{0,1:T(8,128)(2,1)}, u32[]{:S(2)}) copy-start(bf16[1024,320]{0,1:T(8,128)(2,1)} %param.24) | copy-start | bytes 1966084
  7.2 12.8 %copy-start.39 = (bf16[320,256]{1,0:T(8,128)(2,1)S(1)}, bf16[320,256]{1,0:T(8,128)(2,1)}, u32[]{:S(2)}) copy-start(bf16[320,256]{1,0:T(8,128)(2,1)} %param.20) | copy-start | bytes 491524
  7.2 49.6 %reduce-scatter.9.cloned.1.call-start = ((), (), s32[]{:S(2)}) async-start(), calls=%async_computation.8 | async-start | bytes 3145728 | tf_op jit(solution)/shard_map/reduce_scatter | solution.py:75
  14.8 8.1 %copy-start.48 = (f32[256,1]{0,1:T(1,128)}, f32[256,1]{0,1:T(1,128)S(1)}, u32[]{:S(2)}) copy-start(f32[256,1]{0,1:T(1,128)S(1)} %get-tuple-element.91) | copy-start | bytes 3076
  17.9 5.0 copy-start.21
  20.9 2.2 copy-start.47
  23.0 36.9 %copy-start.50 = (f32[256]{0:T(256)S(1)}, f32[256]{0:T(256)}, u32[]{:S(2)}) copy-start(f32[256]{0:T(256)} %param.30) | copy-start | bytes 3076
  23.0 58.1 %reduce-scatter.11.cloned.1.call-start = ((), (), s32[]{:S(2)}) async-start(), calls=%async_computation.9 | async-start | bytes 983040 | tf_op jit(solution)/shard_map/reduce_scatter | solution.py:81
  24.7 35.9 %copy-start.66 = (f32[128]{0:T(128)}, f32[128]{0:T(128)S(1)}, u32[]{:S(2)}) copy-start(f32[128]{0:T(128)S(1)} %negate_power_fusion) | copy-start | bytes 1540
  24.9 35.7 %copy-start.52 = (f32[256]{0:T(256)}, f32[256]{0:T(256)S(1)}, u32[]{:S(2)}) copy-start(f32[256]{0:T(256)S(1)} %fusion.41) | copy-start | bytes 3076
  25.0 36.7 %copy-start.33 = (pred[256,256]{0,1:T(8,128)(4,1)}, pred[256,256]{0,1:T(8,128)(4,1)S(1)}, u32[]{:S(2)}) copy-start(pred[256,256]{0,1:T(8,128)(4,1)S(1)} %fusion.20) | copy-start | bytes 196612
  56.8 3.1 copy-start.15
  58.0 2.7 copy-start.56
  61.3 10.4 %copy-start.29 = (bf16[512,320]{0,1:T(8,128)(2,1)S(1)}, bf16[512,320]{0,1:T(8,128)(2,1)}, u32[]{:S(2)}) copy-start(bf16[512,320]{0,1:T(8,128)(2,1)} %param.21) | copy-start | bytes 983044
  61.7 11.3 %copy-start.64 = (f32[2,256]{1,0:T(2,128)}, f32[2,256]{1,0:T(2,128)S(1)}, u32[]{:S(2)}) copy-start(f32[2,256]{1,0:T(2,128)S(1)} %get-tuple-element.119) | copy-start | bytes 6148
  72.9 14.2 %copy-start.2 = (f32[256,320]{0,1:T(8,128)S(1)}, f32[256,320]{0,1:T(8,128)}, u32[]{:S(2)}) copy-start(f32[256,320]{0,1:T(8,128)} %param.16) | copy-start | bytes 983044
  72.9 14.2 %copy-start.45 = (f32[320]{0:T(512)S(1)}, f32[320]{0:T(512)}, u32[]{:S(2)}) copy-start(f32[320]{0:T(512)} %param.26) | copy-start | bytes 3844
  73.0 20.2 %copy-start.44 = (f32[320]{0:T(512)S(1)}, f32[320]{0:T(512)}, u32[]{:S(2)}) copy-start(f32[320]{0:T(512)} %param.27) | copy-start | bytes 3844
  73.0 82.0 %reduce-scatter.13.cloned.1.call-start = ((), (), s32[]{:S(2)}) async-start(), calls=%async_computation.10 | async-start | bytes 6291456 | tf_op jit(solution)/shard_map/reduce_scatter | solution.py:222
  75.3 24.0 %copy-start.19 = (bf16[320,2048]{1,0:T(8,128)(2,1)}, bf16[320,2048]{1,0:T(8,128)(2,1)S(1)}, u32[]{:S(2)}) copy-start(bf16[320,2048]{1,0:T(8,128)(2,1)S(1)} %constant_dynamic-update-slice_fusion.3) | copy-start | bytes 3932164
  88.2 114.4 %copy-start.4 = (f32[256,320]{0,1:T(8,128)}, f32[256,320]{0,1:T(8,128)S(1)}, u32[]{:S(2)}) copy-start(f32[256,320]{0,1:T(8,128)S(1)} %get-tuple-element.100) | copy-start | bytes 983044
  99.3 79.8 %all-gather.4.cloned.1.call-start = ((), (), s32[]{:S(2)}) async-start(), calls=%async_computation.11 | async-start | bytes 1572864 | tf_op jit(solution)/shard_map/all_gather | solution.py:65
  157.7 38.2 %copy-start.17 = (f32[256,320]{0,1:T(8,128)S(1)}, f32[256,320]{0,1:T(8,128)}, u32[]{:S(2)}) copy-start(f32[256,320]{0,1:T(8,128)} %param.31) | copy-start | bytes 983044
  157.7 38.2 %copy-start.58 = (f32[320]{0:T(512)S(1)}, f32[320]{0:T(512)}, u32[]{:S(2)}) copy-start(f32[320]{0:T(512)} %param.28) | copy-start | bytes 3844
  157.7 32.2 %reduce-scatter.15.cloned.1.call-start = ((), (), s32[]{:S(2)}) async-start(), calls=%async_computation.12 | async-start | bytes 983040 | tf_op jit(solution)/shard_map/reduce_scatter | solution.py:81
  181.8 60.7 %reduce-scatter.17.cloned.1.call-start = ((), (), s32[]{:S(2)}) async-start(), calls=%async_computation.13 | async-start | bytes 3145728 | tf_op jit(solution)/shard_map/reduce_scatter | solution.py:75
  207.2 35.3 %copy-start.1 = (f32[256,2048]{1,0:T(8,128)S(1)}, f32[256,2048]{1,0:T(8,128)}, u32[]{:S(2)}) copy-start(f32[256,2048]{1,0:T(8,128)} %reduce-scatter.13.cloned.1.call-done) | copy-start | bytes 6291460
  209.3 69.6 %all-gather.6.cloned.1.call-start = ((), (), s32[]{:S(2)}) async-start(), calls=%async_computation.14 | async-start | bytes 3145728 | tf_op jit(solution)/shard_map/all_gather | solution.py:239
  244.5 34.4 %copy-start.20 = (bf16[320,2048]{1,0:T(8,128)(2,1)S(1)}, bf16[320,2048]{1,0:T(8,128)(2,1)}, u32[]{:S(2)}) copy-start(bf16[320,2048]{1,0:T(8,128)(2,1)} %copy-done.19) | copy-start | bytes 3932164
  245.6 44.8 %copy-start.5 = (f32[256,320]{0,1:T(8,128)S(1)}, f32[256,320]{0,1:T(8,128)}, u32[]{:S(2)}) copy-start(f32[256,320]{0,1:T(8,128)} %copy-done.4) | copy-start | bytes 983044
  245.7 51.4 %copy-start.6 = (f32[256,320]{0,1:T(8,128)S(1)}, f32[256,320]{0,1:T(8,128)}, u32[]{:S(2)}) copy-start(f32[256,320]{0,1:T(8,128)} %reduce-scatter.11.cloned.1.call-done) | copy-start | bytes 983044
  245.7 51.4 %copy-start.18 = (f32[256,320]{0,1:T(8,128)S(1)}, f32[256,320]{0,1:T(8,128)}, u32[]{:S(2)}) copy-start(f32[256,320]{0,1:T(8,128)} %param.31) | copy-start | bytes 983044
  245.7 44.7 %reduce-scatter.19.cloned.1.call-start = ((), (), s32[]{:S(2)}) async-start(), calls=%async_computation.15 | async-start | bytes 983040 | tf_op jit(solution)/shard_map/reduce_scatter | solution.py:81
  282.2 48.1 %reduce-scatter.21.cloned.1.call-start = ((), (), s32[]{:S(2)}) async-start(), calls=%async_computation.16 | async-start | bytes 1572864 | tf_op jit(solution)/shard_map/reduce_scatter | solution.py:246
  298.9 9.9 %copy-start.65 = (f32[2,256]{1,0:T(2,128)S(1)}, f32[2,256]{1,0:T(2,128)}, u32[]{:S(2)}) copy-start(f32[2,256]{1,0:T(2,128)} %copy-done.64) | copy-start | bytes 6148
  306.1 27.7 %copy-start.26 = (f32[2,256,256]{1,2,0:T(8,128)S(1)}, f32[2,256,256]{1,2,0:T(8,128)}, u32[]{:S(2)}) copy-start(f32[2,256,256]{1,2,0:T(8,128)} %copy-done.25) | copy-start | bytes 1572868
  306.1 27.7 %copy-start.34 = (pred[256,256]{0,1:T(8,128)(4,1)S(1)}, pred[256,256]{0,1:T(8,128)(4,1)}, u32[]{:S(2)}) copy-start(pred[256,256]{0,1:T(8,128)(4,1)} %copy-done.33) | copy-start | bytes 196612
  308.6 27.2 %copy-start.16 = (f32[256,1024]{1,0:T(8,128)S(1)}, f32[256,1024]{1,0:T(8,128)}, u32[]{:S(2)}) copy-start(f32[256,1024]{1,0:T(8,128)} %reduce-scatter.9.cloned.1.call-done) | copy-start | bytes 3145732
  308.6 58.8 %all-gather.8.cloned.1.call-start = ((), (), s32[]{:S(2)}) async-start(), calls=%async_computation.17 | async-start | bytes 1572864 | tf_op jit(solution)/shard_map/all_gather | solution.py:65
  333.8 3.4 copy-start.41
  333.9 3.4 copy-start.43
  335.8 1.7 copy-start.38
  335.8 2.0 copy-start.53
  335.8 2.0 copy-start.67
  337.1 2.0 copy-start.55
  337.5 5.1 copy-start.57
  342.6 24.8 %copy-start.12 = (bf16[320,1024]{1,0:T(8,128)(2,1)S(1)}, bf16[320,1024]{1,0:T(8,128)(2,1)}, u32[]{:S(2)}) copy-start(bf16[320,1024]{1,0:T(8,128)(2,1)} %copy-done.11) | copy-start | bytes 1966084
  343.9 26.1 %copy-start.9 = (bf16[512,1024]{1,0:T(8,128)(2,1)S(1)}, bf16[512,1024]{1,0:T(8,128)(2,1)}, u32[]{:S(2)}) copy-start(bf16[512,1024]{1,0:T(8,128)(2,1)} %all-gather.4.cloned.1.call-done) | copy-start | bytes 3145732
  343.9 26.1 %copy-start.24 = (bf16[512,320]{0,1:T(8,128)(2,1)S(1)}, bf16[512,320]{0,1:T(8,128)(2,1)}, u32[]{:S(2)}) copy-start(bf16[512,320]{0,1:T(8,128)(2,1)} %copy-done.23) | copy-start | bytes 983044
  346.0 76.7 %reduce-scatter.23.cloned.1.call-start = ((), (), s32[]{:S(2)}) async-start(), calls=%async_computation.18 | async-start | bytes 983040 | tf_op jit(solution)/shard_map/reduce_scatter | solution.py:81
  370.0 199.8 %all-reduce.13.cloned.1.call-start = ((), (), s32[]{:S(2)}) async-start(), calls=%async_computation.20 | async-start | bytes 10485760 | tf_op jit(solution)/shard_map/psum | solution.py:269
  370.0 1.9 copy-start.27
  371.9 2.4 copy-start.8
  371.9 3.6 copy-start.22
  376.9 45.7 %copy-start.46 = (f32[320]{0:T(512)S(1)}, f32[320]{0:T(512)}, u32[]{:S(2)}) copy-start(f32[320]{0:T(512)} %param.25) | copy-start | bytes 3844
  376.9 45.7 %copy-start.49 = (f32[256,1]{0,1:T(1,128)S(1)}, f32[256,1]{0,1:T(1,128)}, u32[]{:S(2)}) copy-start(f32[256,1]{0,1:T(1,128)} %copy-done.48) | copy-start | bytes 3076
  377.0 45.7 %copy-start.3 = (f32[256,320]{0,1:T(8,128)S(1)}, f32[256,320]{0,1:T(8,128)}, u32[]{:S(2)}) copy-start(f32[256,320]{0,1:T(8,128)} %param.16) | copy-start | bytes 983044
  377.0 52.3 %copy-start.63 = (f32[256,1]{0,1:T(1,128)S(1)}, f32[256,1]{0,1:T(1,128)}, u32[]{:S(2)}) copy-start(f32[256,1]{0,1:T(1,128)} %get-tuple-element.90) | copy-start | bytes 3076
  377.0 54.1 %copy-start.59 = (f32[320]{0:T(512)S(1)}, f32[320]{0:T(512)}, u32[]{:S(2)}) copy-start(f32[320]{0:T(512)} %get-tuple-element.70) | copy-start | bytes 3844
  377.0 54.1 %copy-start.60 = (f32[320]{0:T(512)S(1)}, f32[320]{0:T(512)}, u32[]{:S(2)}) copy-start(f32[320]{0:T(512)} %get-tuple-element.72) | copy-start | bytes 3844
  377.0 54.1 %copy-start.61 = (f32[320]{0:T(512)S(1)}, f32[320]{0:T(512)}, u32[]{:S(2)}) copy-start(f32[320]{0:T(512)} %get-tuple-element.74) | copy-start | bytes 3844
  377.0 287.6 %all-reduce.11.cloned.1.call-start = ((), (), s32[]{:S(2)}) async-start(), calls=%async_computation.19 | async-start | bytes 1310720 | tf_op jit(solution)/shard_map/psum | solution.py:272
  573.3 96.7 %copy-start.32 = (f32[512,320]{0,1:T(8,128)S(1)}, f32[512,320]{0,1:T(8,128)}, u32[]{:S(2)}) copy-start(f32[512,320]{0,1:T(8,128)} %get-tuple-element.128) | copy-start | bytes 1966084
  573.3 97.6 %copy-start.28 = (f32[1024,320]{0,1:T(8,128)S(1)}, f32[1024,320]{0,1:T(8,128)}, u32[]{:S(2)}) copy-start(f32[1024,320]{0,1:T(8,128)} %get-tuple-element.131) | copy-start | bytes 3932164
  (17 other events, 17.7 us)
Sparse Core Ops, SparseCore 0:
  23.1 33.6 reduce-scatter.8
  73.1 8.0 reduce-scatter.10
  99.4 55.5 reduce-scatter.12
  157.9 21.2 all-gather.3
  181.9 8.0 reduce-scatter.14
  209.4 33.0 reduce-scatter.16
  245.8 33.0 all-gather.5
  282.3 8.0 reduce-scatter.18
  308.7 21.4 reduce-scatter.20
  346.1 21.2 all-gather.7
  370.2 8.0 reduce-scatter.22
  383.4 186.3 all-reduce.12
  573.8 90.7 all-reduce.10
where the time goes:
time: 680 us; the launch traced here: 678 us
  waiting for transfers between devices  436 us (64%)
  blocking collectives  135 us (20%)
  other arithmetic  32.6 us (5%)
  matrix products  29.4 us (4%)
  local copies, waits for them, and re-layouts  28.5 us (4%)
  between operations  15.3 us (2%)
    psum x1, waiting for transfers between devices, on_device(): lax.psum((query_part_grad, out_grad, mix_grad, down_grad), 'dp')  105 us
    psum x1, waiting for transfers between devices, on_device(): lax.psum((key_part_grad, value_part_grad, input_part, attn_part, pre_part...  91.3 us
    reduce_scatter x2, waiting for transfers between devices, project_sum(): lax.psum_scatter(rows_term(gathered, weight, contract), 'row', scatter_di...  64.9 us
    reduce_scatter x1, waiting for transfers between devices, on_device(): lax.psum_scatter(rows_term(ffn_all, mix_weight, 0), 'row', scatter_dimens...  55.6 us
    psum x1, blocking collectives, on_device(): lax.psum((query_gain_part, key_gain_part), ('dp', 'row', 'col'))  44.1 us
    all_gather x2, waiting for transfers between devices, hidden_gather(): return lax.all_gather(values, 'row', axis=0, tiled=True)  42.7 us
    psum x8, blocking collectives, width_total(): return lax.psum(values, 'row')  41 us
    psum x1, blocking collectives, on_device(): lax.psum((key_part_grad, value_part_grad, input_part, attn_part, pre_part...  33.6 us
  transfers between devices with their start and end apart: 13, of which 12 were waited for; matrix products, arithmetic and copies ran while one was open for 3% of the time, Pallas kernels for 0%

commit v1 on v0

--- a/solution.py
+++ b/solution.py
@@ -7,6 +7,18 @@
 HD = 256
 eps_norm = 1e-06
 rope_base = 1000000.0
+
+
+def doubled_up(x, axis, dim):
+    ways, here = (lax.axis_size(axis), lax.axis_index(axis))
+    grown, reach = (x, 1)
+    while reach < ways:
+        theirs = lax.ppermute(grown, axis, [(d, d ^ reach) for d in range(ways)])
+        mine_first = jnp.concatenate([grown, theirs], axis=dim)
+        theirs_first = jnp.concatenate([theirs, grown], axis=dim)
+        grown = jnp.where(here & reach == 0, mine_first, theirs_first)
+        reach = 2 * reach
+    return grown
 
 
 def rms_scale(values):
@@ -62,7 +74,7 @@
 
 
 def hidden_gather(values):
-    return lax.all_gather(values, "row", axis=0, tiled=True)
+    return doubled_up(values, "row", 0)
 
 
 def rows_term(gathered, weight, contract):

time: 680 us -> 659 us (0.969)
  waiting for transfers between devices: 436 us -> 419 us
    all_gather x2 -> x0, waiting for transfers between devices: 42.7 us -> none  [hidden_gather(): return lax.all_gather(values, 'row', axis=0, tiled=True)]
    ppermute x0 -> x2, waiting for transfers between devices: none -> 26.3 us  [doubled_up(): theirs = lax.ppermute(grown, axis, [(d, d ^ reach) for d in range(ways)])]
    unnamed x144 -> x164, local copies, waits for them, and re-layouts: 15.5 us -> 14.3 us
where the time goes in v1:
time: 659 us; the launch traced here: 658 us
  waiting for transfers between devices  419 us (64%)
  blocking collectives  135 us (20%)
  other arithmetic  32.1 us (5%)
  matrix products  28.7 us (4%)
  local copies, waits for them, and re-layouts  26.1 us (4%)
  between operations  15.5 us (2%)
    psum x1, waiting for transfers between devices, on_device(): lax.psum((query_part_grad, out_grad, mix_grad, down_grad), 'dp')  104 us
    psum x1, waiting for transfers between devices, on_device(): lax.psum((key_part_grad, value_part_grad, input_part, attn_part, pre_part...  91.3 us
    reduce_scatter x2, waiting for transfers between devices, project_sum(): lax.psum_scatter(rows_term(gathered, weight, contract), 'row', scatter_di...  64.9 us
    reduce_scatter x1, waiting for transfers between devices, on_device(): lax.psum_scatter(rows_term(ffn_all, mix_weight, 0), 'row', scatter_dimens...  55.6 us
    psum x1, blocking collectives, on_device(): lax.psum((query_gain_part, key_gain_part), ('dp', 'row', 'col'))  44.7 us
    psum x8, blocking collectives, width_total(): return lax.psum(values, 'row')  40.9 us
    all_gather x1, waiting for transfers between devices, on_device(): grad_mix_all = lax.all_gather(grad_mix, 'row', axis=0, tiled=True)  33.2 us
    psum x1, blocking collectives, on_device(): lax.psum((key_part_grad, value_part_grad, input_part, attn_part, pre_part...  32.4 us
  transfers between devices with their start and end apart: 13, of which 12 were waited for; matrix products, arithmetic and copies ran while one was open for 3% of the time, Pallas kernels for 0%

profile of v1, /device:TPU:0, one launch (start us, length us, event | category | flops | bytes accessed | tf_op | source)
XLA Modules:
  0.0 658.1 jit_solution(13466384445955721293)
XLA Ops:
  7.3 1.1 multiply_reduce_fusion.14
  8.4 5.9 psum.140
  14.9 1.1 multiply_convert_fusion.4
  16.0 2.0 all_gather.18
  18.0 1.1 constant_dynamic-update-slice_fusion.2
  21.0 2.1 fusion.54
  25.1 31.8 %reduce-scatter.9.cloned.1.call-done = f32[256,1024]{1,0:T(8,128)} async-done(((f32[512,1024]{1,0:T(8,128)}), f32[256,1024]{1,0:T(8,128)}) %reduce-scatter.9.cloned.1.call-update) | async-done | bytes 1048592 | tf_op jit(solution)/shard_map/reduce_scatter | solution.py:87
  56.9 1.1 multiply_reduce_fusion.17
  58.1 1.1 slice.83
  62.5 8.6 %all_gather.19 = bf16[512,512]{0,1:T(8,128)(2,1)S(1)} all-gather(bf16[256,512]{0,1:T(8,128)(2,1)S(1)} %bitcast.103), channel_id=1, replica_groups=mesh['dp'=8,'row'=2,'col'=2] {'row'}, dimensions={0}, use_global_device_ids=true | all-gather | bytes 786432 | tf_op jit(solution)/shard_map/all_gather | solution.py:227
  71.8 1.2 fusion.63
  73.1 1.2 constant_dynamic-update-slice_fusion.4
  74.3 1.1 constant_dynamic-update-slice_fusion.3
  75.4 5.8 reduce-scatter.11.cloned.1.call-done
  82.3 4.9 psum.141
  87.8 1.1 multiply_reduce_fusion.12
  88.9 4.9 psum.142
  94.5 2.0 all_gather.20
  97.3 3.2 fusion.55
  100.6 55.6 %reduce-scatter.13.cloned.1.call-done = f32[256,2048]{1,0:T(8,128)} async-done(((f32[512,2048]{1,0:T(8,128)}), f32[256,2048]{1,0:T(8,128)}) %reduce-scatter.13.cloned.1.call-update) | async-done | bytes 2097168 | tf_op jit(solution)/shard_map/reduce_scatter | solution.py:234
  156.2 1.9 multiply_convert_fusion.1
  158.5 13.2 %collective-permute-done = bf16[256,1024]{1,0:T(8,128)(2,1)S(1)} collective-permute-done((bf16[256,1024]{1,0:T(8,128)(2,1)S(1)}, bf16[256,1024]{1,0:T(8,128)(2,1)S(1)}, u32[]{:S(2)}, u32[]{:S(2)}) %collective-permute-start) | collective-permute-done | bytes 524320 | tf_op jit(solution)/shard_map/ppermute | solution.py:16
  171.7 1.4 fusion.32
  173.2 8.1 %reduce-scatter.15.cloned.1.call-done = f32[256,320]{0,1:T(8,128)} async-done(((f32[512,320]{0,1:T(8,128)}), f32[256,320]{0,1:T(8,128)}) %reduce-scatter.15.cloned.1.call-update) | async-done | bytes 327696 | tf_op jit(solution)/shard_map/reduce_scatter | solution.py:93
  182.3 4.9 psum.143
  187.3 1.8 multiply_reduce_fusion.3
  189.0 4.9 psum.144
  194.0 1.8 subtract_convert_fusion.1
  195.8 2.0 all_gather.21
  198.6 2.1 fusion.56
  200.7 33.2 %reduce-scatter.17.cloned.1.call-done = f32[256,1024]{1,0:T(8,128)} async-done(((f32[512,1024]{1,0:T(8,128)}), f32[256,1024]{1,0:T(8,128)}) %reduce-scatter.17.cloned.1.call-update) | async-done | bytes 1048592 | tf_op jit(solution)/shard_map/reduce_scatter | solution.py:87
  233.9 2.0 fusion.10
  235.9 1.1 pad_maximum_fusion
  237.1 33.2 %all-gather.2.cloned.1.call-done = bf16[512,2048]{1,0:T(8,128)(2,1)} async-done(((bf16[256,2048]{1,0:T(8,128)(2,1)}), bf16[512,2048]{1,0:T(8,128)(2,1)}) %all-gather.2.cloned.1.call-update) | async-done | bytes 2097168 | tf_op jit(solution)/shard_map/all_gather | solution.py:251
  270.2 3.3 fusion.57
  273.6 8.1 %reduce-scatter.19.cloned.1.call-done = f32[256,320]{0,1:T(8,128)} async-done(((f32[512,320]{0,1:T(8,128)}), f32[256,320]{0,1:T(8,128)}) %reduce-scatter.19.cloned.1.call-update) | async-done | bytes 327696 | tf_op jit(solution)/shard_map/reduce_scatter | solution.py:93
  281.8 1.8 multiply_reduce_fusion.4
  283.5 4.9 psum.145
  288.4 1.9 multiply_reduce_fusion.5
  290.3 5.0 psum.146
  295.5 2.0 all_gather.23
  298.2 2.5 fusion.58
  301.0 21.4 %reduce-scatter.21.cloned.1.call-done = f32[256,512]{1,0:T(8,128)} async-done(((f32[512,512]{1,0:T(8,128)}), f32[256,512]{1,0:T(8,128)}) %reduce-scatter.21.cloned.1.call-update) | async-done | bytes 524304 | tf_op jit(solution)/shard_map/reduce_scatter | solution.py:258
  322.4 1.8 convert_element_type.61
  324.1 1.8 copy.135
  325.9 1.9 fusion.3
  327.9 1.2 multiply_reduce_fusion.1
  332.0 1.1 copy.113
  334.8 13.2 %collective-permute-done.1 = bf16[256,1024]{1,0:T(8,128)(2,1)S(1)} collective-permute-done((bf16[256,1024]{1,0:T(8,128)(2,1)S(1)}, bf16[256,1024]{1,0:T(8,128)(2,1)S(1)}, u32[]{:S(2)}, u32[]{:S(2)}) %collective-permute-start.1) | collective-permute-done | bytes 524320 | tf_op jit(solution)/shard_map/ppermute | solution.py:16
  348.0 1.6 maximum_select_fusion.1
  349.6 1.4 fusion.59
  351.0 3.3 fusion.31
  354.3 2.4 fusion.62
  356.7 1.2 fusion.61
  359.5 44.7 %all-reduce.4 = (f32[256]{0:T(256)}, f32[256]{0:T(256)}) all-reduce(f32[256]{0:T(256)S(1)} %get-tuple-element.68, f32[256]{0:T(256)S(1)} %get-tuple-element.56), channel_id=1, replica_groups=mesh['dp'=8,'row'=2,'col'=2] {'dp','row','col'}, use_global_device_ids=true, to_apply=%region_47.48 | all-reduce | flops 512 | bytes 4096 | tf_op jit(solution)/shard_map/psum | solution.py:287
  405.2 1.2 multiply_reduce_fusion.6
  406.4 5.4 psum.147
  411.8 1.8 subtract_add_fusion
  413.6 32.4 %all-reduce.5 = (f32[320]{0:T(512)}, f32[320]{0:T(512)}, f32[320]{0:T(512)}, f32[320]{0:T(512)}) all-reduce(f32[320]{0:T(512)S(1)} %get-tuple-element.76, f32[320]{0:T(512)S(1)} %copy-done.70, f32[320]{0:T(512)S(1)} %copy-done.69, f32[320]{0:T(512)S(1)} %copy-done.68), channel_id=1, replica_groups=mesh['dp'=8,'row'=2,'col'=2] {'dp','col'}, use_global_device_ids=true, to_apply=%region_39.40 | all-reduce | flops 1280 | bytes 10240 | tf_op jit(solution)/shard_map/psum | solution.py:284
  446.1 104.5 %all-reduce.13.cloned.1.call-done = (f32[320,512]{1,0:T(8,128)}, f32[512,320]{0,1:T(8,128)}, f32[320,2048]{1,0:T(8,128)}, f32[1024,320]{0,1:T(8,128)}) async-done(((f32[320,512]{1,0:T(8,128)}, f32[512,320]{0,1:T(8,128)}, f32[320,2048]{1,0:T(8,128)}, f32[1024,320]{0,1:T(8,128)}), (f32[320,512]{1,0:T(8,128)}, f32[512,320]{0,1:T(8,128)}, f32[320,2048]{1,0:T(8,128)}, ...) | async-done | bytes 5242896 | tf_op jit(solution)/shard_map/psum | solution.py:281
  550.6 3.6 fusion.52
  554.2 91.3 %all-reduce.11.cloned.1.call-done = (f32[320,256]{1,0:T(8,128)}, f32[320,256]{1,0:T(8,128)}) async-done(((f32[320,256]{1,0:T(8,128)}, f32[320,256]{1,0:T(8,128)}), (f32[320,256]{1,0:T(8,128)}, f32[320,256]{1,0:T(8,128)})) %all-reduce.11.cloned.1.call-update) | async-done | bytes 655376 | tf_op jit(solution)/shard_map/psum | solution.py:284
  646.3 1.7 copy.151
  648.0 1.7 copy.152
  (231 shorter events, 24.2 us)
Async XLA Ops:
  7.2 164.5 %copy-start = (bf16[1024,320]{0,1:T(8,128)(2,1)S(1)}, bf16[1024,320]{0,1:T(8,128)(2,1)}, u32[]{:S(2)}) copy-start(bf16[1024,320]{0,1:T(8,128)(2,1)} %param.24) | copy-start | bytes 1966084
  7.2 12.9 %copy-start.42 = (bf16[320,256]{1,0:T(8,128)(2,1)S(1)}, bf16[320,256]{1,0:T(8,128)(2,1)}, u32[]{:S(2)}) copy-start(bf16[320,256]{1,0:T(8,128)(2,1)} %param.20) | copy-start | bytes 491524
  7.2 49.7 %reduce-scatter.9.cloned.1.call-start = ((), (), s32[]{:S(2)}) async-start(), calls=%async_computation.8 | async-start | bytes 3145728 | tf_op jit(solution)/shard_map/reduce_scatter | solution.py:87
  21.0 2.1 copy-start.52
  23.0 36.9 %copy-start.58 = (f32[256]{0:T(256)S(1)}, f32[256]{0:T(256)}, u32[]{:S(2)}) copy-start(f32[256]{0:T(256)} %param.30) | copy-start | bytes 3076
  23.1 58.2 %reduce-scatter.11.cloned.1.call-start = ((), (), s32[]{:S(2)}) async-start(), calls=%async_computation.9 | async-start | bytes 983040 | tf_op jit(solution)/shard_map/reduce_scatter | solution.py:93
  24.8 35.9 %copy-start.75 = (f32[128]{0:T(128)}, f32[128]{0:T(128)S(1)}, u32[]{:S(2)}) copy-start(f32[128]{0:T(128)S(1)} %negate_power_fusion) | copy-start | bytes 1540
  25.0 35.7 %copy-start.61 = (f32[256]{0:T(256)}, f32[256]{0:T(256)S(1)}, u32[]{:S(2)}) copy-start(f32[256]{0:T(256)S(1)} %fusion.43) | copy-start | bytes 3076
  56.9 3.1 copy-start.13
  58.0 2.7 copy-start.65
  58.1 2.8 copy-start.50
  61.4 10.5 %copy-start.30 = (bf16[512,320]{0,1:T(8,128)(2,1)S(1)}, bf16[512,320]{0,1:T(8,128)(2,1)}, u32[]{:S(2)}) copy-start(bf16[512,320]{0,1:T(8,128)(2,1)} %param.21) | copy-start | bytes 983044
  61.7 11.3 %copy-start.73 = (f32[2,256]{1,0:T(2,128)}, f32[2,256]{1,0:T(2,128)S(1)}, u32[]{:S(2)}) copy-start(f32[2,256]{1,0:T(2,128)S(1)} %get-tuple-element.119) | copy-start | bytes 6148
  73.0 14.8 %copy-start.2 = (f32[256,320]{0,1:T(8,128)S(1)}, f32[256,320]{0,1:T(8,128)}, u32[]{:S(2)}) copy-start(f32[256,320]{0,1:T(8,128)} %param.16) | copy-start | bytes 983044
  73.0 14.8 %copy-start.48 = (f32[320]{0:T(512)S(1)}, f32[320]{0:T(512)}, u32[]{:S(2)}) copy-start(f32[320]{0:T(512)} %param.26) | copy-start | bytes 3844
  73.0 21.4 %copy-start.47 = (f32[320]{0:T(512)S(1)}, f32[320]{0:T(512)}, u32[]{:S(2)}) copy-start(f32[320]{0:T(512)} %param.27) | copy-start | bytes 3844
  73.1 83.2 %reduce-scatter.13.cloned.1.call-start = ((), (), s32[]{:S(2)}) async-start(), calls=%async_computation.10 | async-start | bytes 6291456 | tf_op jit(solution)/shard_map/reduce_scatter | solution.py:234
  75.4 25.1 %copy-start.17 = (bf16[320,2048]{1,0:T(8,128)(2,1)}, bf16[320,2048]{1,0:T(8,128)(2,1)S(1)}, u32[]{:S(2)}) copy-start(bf16[320,2048]{1,0:T(8,128)(2,1)S(1)} %constant_dynamic-update-slice_fusion.3) | copy-start | bytes 3932164
  87.8 12.8 %copy-start.56 = (f32[256,1]{0,1:T(1,128)}, f32[256,1]{0,1:T(1,128)S(1)}, u32[]{:S(2)}) copy-start(f32[256,1]{0,1:T(1,128)S(1)} %get-tuple-element.93) | copy-start | bytes 3076
  88.9 105.1 %copy-start.4 = (f32[256,320]{0,1:T(8,128)}, f32[256,320]{0,1:T(8,128)S(1)}, u32[]{:S(2)}) copy-start(f32[256,320]{0,1:T(8,128)S(1)} %get-tuple-element.100) | copy-start | bytes 983044
  94.4 6.1 copy-start.55
  100.6 80.7 %reduce-scatter.15.cloned.1.call-start = ((), (), s32[]{:S(2)}) async-start(), calls=%async_computation.11 | async-start | bytes 983040 | tf_op jit(solution)/shard_map/reduce_scatter | solution.py:93
  158.1 15.0 %copy-start.37 = (bf16[256,1024]{1,0:T(8,128)(2,1)}, bf16[256,1024]{1,0:T(8,128)(2,1)S(1)}, u32[]{:S(2)}) copy-start(bf16[256,1024]{1,0:T(8,128)(2,1)S(1)} %multiply_convert_fusion.1) | copy-start | bytes 1572868
  158.1 13.6 %collective-permute-start = (bf16[256,1024]{1,0:T(8,128)(2,1)S(1)}, bf16[256,1024]{1,0:T(8,128)(2,1)S(1)}, u32[]{:S(2)}, u32[]{:S(2)}) collective-permute-start(bf16[256,1024]{1,0:T(8,128)(2,1)S(1)} %multiply_convert_fusion.1), channel_id=1, source_target_pairs={{0,2},{2,0},{1,3},{3,1},{4,6},{6,4},{5,7},{7,5},{8,10},{10,8},{9,1... | collective-permute-start | bytes 1572872 | tf_op jit(solution)/shard_map/ppermute | solution.py:16
  158.5 28.7 %copy-start.15 = (f32[256,320]{0,1:T(8,128)S(1)}, f32[256,320]{0,1:T(8,128)}, u32[]{:S(2)}) copy-start(f32[256,320]{0,1:T(8,128)} %param.31) | copy-start | bytes 983044
  158.5 28.7 %copy-start.67 = (f32[320]{0:T(512)S(1)}, f32[320]{0:T(512)}, u32[]{:S(2)}) copy-start(f32[320]{0:T(512)} %param.28) | copy-start | bytes 3844
  173.1 60.7 %reduce-scatter.17.cloned.1.call-start = ((), (), s32[]{:S(2)}) async-start(), calls=%async_computation.12 | async-start | bytes 3145728 | tf_op jit(solution)/shard_map/reduce_scatter | solution.py:87
  198.6 35.3 %copy-start.1 = (f32[256,2048]{1,0:T(8,128)S(1)}, f32[256,2048]{1,0:T(8,128)}, u32[]{:S(2)}) copy-start(f32[256,2048]{1,0:T(8,128)} %reduce-scatter.13.cloned.1.call-done) | copy-start | bytes 6291460
  200.6 69.6 %all-gather.2.cloned.1.call-start = ((), (), s32[]{:S(2)}) async-start(), calls=%async_computation.13 | async-start | bytes 3145728 | tf_op jit(solution)/shard_map/all_gather | solution.py:251
  235.9 34.3 %copy-start.18 = (bf16[320,2048]{1,0:T(8,128)(2,1)S(1)}, bf16[320,2048]{1,0:T(8,128)(2,1)}, u32[]{:S(2)}) copy-start(bf16[320,2048]{1,0:T(8,128)(2,1)} %copy-done.17) | copy-start | bytes 3932164
  237.0 44.8 %copy-start.5 = (f32[256,320]{0,1:T(8,128)S(1)}, f32[256,320]{0,1:T(8,128)}, u32[]{:S(2)}) copy-start(f32[256,320]{0,1:T(8,128)} %copy-done.4) | copy-start | bytes 983044
  237.0 51.4 %copy-start.6 = (f32[256,320]{0,1:T(8,128)S(1)}, f32[256,320]{0,1:T(8,128)}, u32[]{:S(2)}) copy-start(f32[256,320]{0,1:T(8,128)} %reduce-scatter.11.cloned.1.call-done) | copy-start | bytes 983044
  237.0 51.4 %copy-start.16 = (f32[256,320]{0,1:T(8,128)S(1)}, f32[256,320]{0,1:T(8,128)}, u32[]{:S(2)}) copy-start(f32[256,320]{0,1:T(8,128)} %param.31) | copy-start | bytes 983044
  237.0 44.7 %reduce-scatter.19.cloned.1.call-start = ((), (), s32[]{:S(2)}) async-start(), calls=%async_computation.14 | async-start | bytes 983040 | tf_op jit(solution)/shard_map/reduce_scatter | solution.py:93
  273.5 21.8 %copy-start.57 = (f32[256,1]{0,1:T(1,128)S(1)}, f32[256,1]{0,1:T(1,128)}, u32[]{:S(2)}) copy-start(f32[256,1]{0,1:T(1,128)} %copy-done.56) | copy-start | bytes 3076
  273.5 21.8 %copy-start.71 = (f32[256,1]{0,1:T(1,128)S(1)}, f32[256,1]{0,1:T(1,128)}, u32[]{:S(2)}) copy-start(f32[256,1]{0,1:T(1,128)} %get-tuple-element.92) | copy-start | bytes 3076
  273.6 48.8 %reduce-scatter.21.cloned.1.call-start = ((), (), s32[]{:S(2)}) async-start(), calls=%async_computation.15 | async-start | bytes 1572864 | tf_op jit(solution)/shard_map/reduce_scatter | solution.py:258
  290.3 10.7 %copy-start.74 = (f32[2,256]{1,0:T(2,128)S(1)}, f32[2,256]{1,0:T(2,128)}, u32[]{:S(2)}) copy-start(f32[2,256]{1,0:T(2,128)} %copy-done.73) | copy-start | bytes 6148
  298.2 27.7 %copy-start.25 = (f32[2,256,256]{1,2,0:T(8,128)S(1)}, f32[2,256,256]{1,2,0:T(8,128)}, u32[]{:S(2)}) copy-start(f32[2,256,256]{1,2,0:T(8,128)} %copy-done.24) | copy-start | bytes 1572868
  300.7 27.2 %copy-start.14 = (f32[256,1024]{1,0:T(8,128)S(1)}, f32[256,1024]{1,0:T(8,128)}, u32[]{:S(2)}) copy-start(f32[256,1024]{1,0:T(8,128)} %reduce-scatter.9.cloned.1.call-done) | copy-start | bytes 3145732
  300.7 104.4 %reduce-scatter.23.cloned.1.call-start = ((), (), s32[]{:S(2)}) async-start(), calls=%async_computation.16 | async-start | bytes 983040 | tf_op jit(solution)/shard_map/reduce_scatter | solution.py:93
  325.9 3.4 copy-start.44
  325.9 3.4 copy-start.46
  330.7 2.5 copy-start.60
  333.1 16.5 %copy-start.10 = (bf16[320,1024]{1,0:T(8,128)(2,1)S(1)}, bf16[320,1024]{1,0:T(8,128)(2,1)}, u32[]{:S(2)}) copy-start(bf16[320,1024]{1,0:T(8,128)(2,1)} %copy-done.9) | copy-start | bytes 1966084
  334.4 16.6 %copy-start.29 = (bf16[512,320]{0,1:T(8,128)(2,1)S(1)}, bf16[512,320]{0,1:T(8,128)(2,1)}, u32[]{:S(2)}) copy-start(bf16[512,320]{0,1:T(8,128)(2,1)} %copy-done.28) | copy-start | bytes 983044
  334.4 13.6 %collective-permute-start.1 = (bf16[256,1024]{1,0:T(8,128)(2,1)S(1)}, bf16[256,1024]{1,0:T(8,128)(2,1)S(1)}, u32[]{:S(2)}, u32[]{:S(2)}) collective-permute-start(bf16[256,1024]{1,0:T(8,128)(2,1)S(1)} %pad_maximum_fusion.1), channel_id=1, source_target_pairs={{0,2},{2,0},{1,3},{3,1},{4,6},{6,4},{5,7},{7,5},{8,10},{10,8},{9,1... | collective-permute-start | bytes 1572872 | tf_op jit(solution)/shard_map/ppermute | solution.py:16
  351.0 3.4 copy-start.12
  351.0 199.6 %all-reduce.13.cloned.1.call-start = ((), (), s32[]{:S(2)}) async-start(), calls=%async_computation.18 | async-start | bytes 10485760 | tf_op jit(solution)/shard_map/psum | solution.py:281
  351.0 3.3 copy-start.26
  354.3 2.4 copy-start.8
  354.3 2.4 copy-start.22
  354.3 3.6 copy-start.20
  359.3 45.8 %copy-start.49 = (f32[320]{0:T(512)S(1)}, f32[320]{0:T(512)}, u32[]{:S(2)}) copy-start(f32[320]{0:T(512)} %param.25) | copy-start | bytes 3844
  359.3 45.8 %copy-start.54 = (f32[256,1]{0,1:T(1,128)S(1)}, f32[256,1]{0,1:T(1,128)}, u32[]{:S(2)}) copy-start(f32[256,1]{0,1:T(1,128)} %copy-done.53) | copy-start | bytes 3076
  359.4 45.8 %copy-start.3 = (f32[256,320]{0,1:T(8,128)S(1)}, f32[256,320]{0,1:T(8,128)}, u32[]{:S(2)}) copy-start(f32[256,320]{0,1:T(8,128)} %param.16) | copy-start | bytes 983044
  359.4 52.4 %copy-start.72 = (f32[256,1]{0,1:T(1,128)S(1)}, f32[256,1]{0,1:T(1,128)}, u32[]{:S(2)}) copy-start(f32[256,1]{0,1:T(1,128)} %get-tuple-element.90) | copy-start | bytes 3076
  359.4 54.2 %copy-start.68 = (f32[320]{0:T(512)S(1)}, f32[320]{0:T(512)}, u32[]{:S(2)}) copy-start(f32[320]{0:T(512)} %get-tuple-element.70) | copy-start | bytes 3844
  359.4 54.2 %copy-start.69 = (f32[320]{0:T(512)S(1)}, f32[320]{0:T(512)}, u32[]{:S(2)}) copy-start(f32[320]{0:T(512)} %get-tuple-element.72) | copy-start | bytes 3844
  359.4 54.2 %copy-start.70 = (f32[320]{0:T(512)S(1)}, f32[320]{0:T(512)}, u32[]{:S(2)}) copy-start(f32[320]{0:T(512)} %get-tuple-element.74) | copy-start | bytes 3844
  359.4 286.0 %all-reduce.11.cloned.1.call-start = ((), (), s32[]{:S(2)}) async-start(), calls=%async_computation.17 | async-start | bytes 1310720 | tf_op jit(solution)/shard_map/psum | solution.py:284
  550.6 94.9 %copy-start.36 = (f32[320,512]{1,0:T(8,128)S(1)}, f32[320,512]{1,0:T(8,128)}, u32[]{:S(2)}) copy-start(f32[320,512]{1,0:T(8,128)} %get-tuple-element.125) | copy-start | bytes 1966084
  554.1 95.5 %copy-start.35 = (f32[512,320]{0,1:T(8,128)S(1)}, f32[512,320]{0,1:T(8,128)}, u32[]{:S(2)}) copy-start(f32[512,320]{0,1:T(8,128)} %get-tuple-element.128) | copy-start | bytes 1966084
  554.2 96.4 %copy-start.27 = (f32[1024,320]{0,1:T(8,128)S(1)}, f32[1024,320]{0,1:T(8,128)}, u32[]{:S(2)}) copy-start(f32[1024,320]{0,1:T(8,128)} %get-tuple-element.131) | copy-start | bytes 3932164
  (27 other events, 34.5 us)
Sparse Core Ops, SparseCore 0:
  23.2 33.6 reduce-scatter.8
  73.2 8.0 reduce-scatter.10
  100.7 55.4 reduce-scatter.12
  173.2 8.0 reduce-scatter.14
  200.8 33.0 reduce-scatter.16
  237.1 33.0 all-gather.1
  273.7 8.0 reduce-scatter.18
  300.8 21.4 reduce-scatter.20
  351.1 8.0 reduce-scatter.22
  364.2 186.2 all-reduce.12
  554.6 90.7 all-reduce.10
